TPU v7x, 32 devices: a whole 2x2x4 slice. The times are simulated.
32 devices in a mesh: group: 8 (over z, core), dp: 4 (over y, x).
Axes of the slice: x: 2, y: 2, z: 4, core: 2. Of those that a mesh axis runs over, the one named last changes fastest.
Arguments:
- resp_q: bfloat16 [8, 1024, 4096], P('group', 'dp'), may hold values from -410 to 410
- resp_k: bfloat16 [8, 1024, 4096], P('group', 'dp'), may hold values from -410 to 410
- resp_v: bfloat16 [8, 1024, 4096], P('group', 'dp'), may hold values from -6 to 6
- prompt_k: bfloat16 [8, 512, 4096], P('group', 'dp'), may hold values from -410 to 410
- prompt_v: bfloat16 [8, 512, 4096], P('group', 'dp'), may hold values from -6 to 6
- prompt_len: int32 [8], P('group'), may hold values from 128 to 512
- resp_len: int32 [8, 4], P('group', 'dp'), may hold values from 1 to 256, as said below
- assign: int32 [8, 8], P('group', 'dp'), may hold values from 0 to 15, as said below
- rewards: float32 [8, 4], P('group', 'dp'), may hold values from -18 to 18
- feat_q: bfloat16 [32, 128, 128], replicated, may hold values from -1 to 1
- feat_k: bfloat16 [32, 128, 128], replicated, may hold values from -1 to 1
Outputs:
- attn_out: bfloat16 [8, 512, 4096], P('group', 'dp')
- token_adv: float32 [8, 512], P('group', 'dp')
Inputs may be any that keep to these rules, and one draw needn't show every extreme that they name: Response r of a prompt has ceil(resp_len / 64) live blocks; these counts sum to 2 * 4 over a prompt's responses, and one response of every prompt has 4 blocks. `assign`: entry d * 2 + j names the block r * 4 + c (block c of response r) whose outputs go to slot j of device d of dp. Every live block of the prompt is named exactly once, and the 2 slots of one device name blocks of different responses.
All inputs are finite; a program needn't handle non-finite values.
Results may differ from a plain program's by a relative error of at most 0.0085.
Values may be sent and summed in bfloat16 or wider, within the bound.
A program may use at most 128 MiB of HBM per device.

v0:
```python
import jax
import jax.numpy as jnp
from jax import lax
from jax.sharding import PartitionSpec as P

BLK = 64


def features(rows, weights):
    logits = jnp.einsum("thd,hdf->thf", rows, weights, preferred_element_type=jnp.float32)
    return jnp.concatenate(
        [jax.nn.softmax(logits, axis=-1), jax.nn.softmax(-logits, axis=-1)], axis=-1
    ).astype(jnp.bfloat16)


def state_terms(query_feat, state_rounded, total_rounded):
    numerator = jnp.einsum(
        "thf,hfe->the", query_feat, state_rounded, preferred_element_type=jnp.float32
    )
    denominator = jnp.einsum(
        "thf,hf->th", query_feat, total_rounded, preferred_element_type=jnp.float32
    )
    return (numerator.astype(jnp.bfloat16), denominator.astype(jnp.bfloat16))


def body(
    resp_q,
    resp_k,
    resp_v,
    prompt_k,
    prompt_v,
    prompt_len,
    resp_len,
    assign,
    rewards,
    feat_q,
    feat_k,
):
    dp_count = lax.axis_size("dp")
    my_index = lax.axis_index("dp")
    head_count = feat_q.shape[0]
    head_width = feat_q.shape[1]
    length = resp_q.shape[1]
    prompt_rows = prompt_k.shape[1]
    queries = resp_q[0].reshape(length, head_count, head_width)
    key_rows = resp_k[0].reshape(length, head_count, head_width)
    values = resp_v[0].reshape(length, head_count, head_width)
    prompt_keys = prompt_k[0].reshape(prompt_rows, head_count, head_width)
    prompt_values = prompt_v[0].reshape(prompt_rows, head_count, head_width)
    keep = my_index * prompt_rows + jnp.arange(prompt_rows) < prompt_len[0]
    prompt_feat = jnp.where(
        keep[:, None, None], features(prompt_keys, feat_k), jnp.zeros((), jnp.bfloat16)
    )
    part_state = jnp.einsum(
        "shf,she->hfe", prompt_feat, prompt_values, preferred_element_type=jnp.float32
    )
    part_total = jnp.sum(prompt_feat.astype(jnp.float32), axis=0)
    query_feat = features(queries, feat_q)
    key_feat = features(key_rows, feat_k)
    kv_share, total_share = (
        lax.psum_scatter(part_state, "dp", scatter_dimension=0, tiled=True),
        lax.psum_scatter(part_total, "dp", scatter_dimension=0, tiled=True),
    )
    kv_state, key_total = (
        lax.all_gather(kv_share.astype(jnp.bfloat16), "dp", axis=0, tiled=True),
        lax.all_gather(total_share.astype(jnp.bfloat16), "dp", axis=0, tiled=True),
    )
    prompt_num, prompt_den = state_terms(query_feat, kv_state, key_total)
    causal = jnp.arange(length)[:, None] >= jnp.arange(length)[None, :]
    scores = jnp.einsum("thf,shf->hts", query_feat, key_feat, preferred_element_type=jnp.float32)
    scores = jnp.where(causal[None], scores, jnp.float32(0.0))
    intra_den = jnp.sum(scores, axis=-1)
    intra_num = jnp.einsum(
        "hts,she->the", scores.astype(jnp.bfloat16), values, preferred_element_type=jnp.float32
    )
    combined = (prompt_num.astype(jnp.float32) + intra_num) / (
        prompt_den.astype(jnp.float32) + intra_den.T
    )[:, :, None]
    live_rows = jnp.arange(length) < resp_len[0, 0]
    combined = jnp.where(live_rows[:, None, None], combined, jnp.float32(0.0))
    result = combined.astype(jnp.bfloat16).reshape(-1, BLK, head_count * head_width)
    pieces = result.shape[0]
    slot_width = assign.shape[1]
    table, lengths = (
        lax.all_gather(assign, "dp", axis=1, tiled=True),
        lax.all_gather(resp_len, "dp", axis=1, tiled=True),
    )
    slot_ids = table[0].reshape(dp_count, slot_width)
    own_ids = assign[0]
    source = own_ids // pieces
    stretch_index = own_ids % pieces
    picker = source[:, None] == jnp.arange(dp_count)[None, :]
    mine_mask = jnp.any(
        slot_ids[:, :, None] == my_index * pieces + jnp.arange(pieces)[None, None, :], axis=1
    )
    outgoing = jnp.einsum(
        "dc,cbe->dbe", mine_mask.astype(jnp.bfloat16), result, preferred_element_type=jnp.float32
    ).astype(jnp.bfloat16)
    incoming = lax.all_to_all(outgoing, "dp", split_axis=0, concat_axis=0, tiled=True)
    attended = jnp.einsum(
        "jd,dbe->jbe", picker.astype(jnp.bfloat16), incoming, preferred_element_type=jnp.float32
    ).astype(jnp.bfloat16)
    attended = attended.reshape(1, slot_width * BLK, head_count * head_width)
    reward_all = lax.all_gather(rewards, "dp", axis=1, tiled=True)[0]
    centred = reward_all - jnp.sum(reward_all) / dp_count
    spread = lax.psum(jnp.sum(centred * centred), "group")
    advantage = centred / jnp.sqrt(spread / (lax.axis_size("group") * dp_count) + 1e-06)
    slot_adv = jnp.sum(jnp.where(picker, advantage[None, :], jnp.float32(0.0)), axis=1)
    slot_len = jnp.sum(jnp.where(picker, lengths[0][None, :], 0), axis=1)
    positions = stretch_index[:, None] * BLK + jnp.arange(BLK)[None, :]
    token_adv = jnp.where(positions < slot_len[:, None], slot_adv[:, None], jnp.float32(0.0))
    return (attended, token_adv.reshape(1, slot_width * BLK))


def solution(mesh):
    return jax.shard_map(
        body,
        mesh=mesh,
        in_specs=(
            P("group", "dp", None),
            P("group", "dp", None),
            P("group", "dp", None),
            P("group", "dp", None),
            P("group", "dp", None),
            P("group"),
            P("group", "dp"),
            P("group", "dp"),
            P("group", "dp"),
            P(),
            P(),
        ),
        out_specs=(P("group", "dp", None), P("group", "dp")),
        check_vma=False,
    )
```

profile of v0, /device:TPU:0, one launch (start us, length us, event | category | flops | bytes accessed | tf_op | source)
XLA Modules:
  0.0 187.2 jit_solution(10308482313674577774)
XLA Ops:
  7.2 1.5 copy.91
  8.8 2.5 %fusion.63 = (f32[128,32]{0,1:T(8,128)S(1)}, f32[128,32,128]{0,2,1:T(8,128)}) fusion(bf16[32,128,128]{2,1,0:T(8,128)(2,1)S(1)} %copy-done, bf16[128,32,128]{2,1,0:T(8,128)(2,1)S(1)} %bitcast.135), kind=kOutput, calls=%fused_computation.102 | convolution fusion | flops 135790720 | bytes 4210688 | tf_op jit(solution)/shard_map/sub | solution.py:12
  11.3 0.9 fusion.40
  12.1 1.9 %fusion.66 = (f32[128,32]{0,1:T(8,128)S(1)}, f32[128,32,128]{0,2,1:T(8,128)S(1)}) fusion(f32[32,128,128]{2,1,0:T(8,128)S(1)} %fusion.40), kind=kOutput, calls=%fused_computation.103 | output fusion | flops 1048703 | bytes 4210688 | tf_op jit(solution)/shard_map/sub | solution.py:12
  14.7 2.4 %copy.92 = bf16[16,8,32,128]{3,2,1,0:T(8,128)(2,1)} copy(bf16[16,8,32,128]{3,1,2,0:T(8,128)(2,1)} %bitcast.142) | data formatting | bytes 2097152
  17.2 2.3 %divide_convert_fusion.4 = (bf16[128,32,128]{0,2,1:T(8,128)(2,1)S(1)}, bf16[128,32,128]{0,2,1:T(8,128)(2,1)S(1)}) fusion(f32[128,32,128]{0,2,1:T(8,128)} %get-tuple-element.22, f32[128,32]{0,1:T(8,128)S(1)} %get-tuple-element.21, f32[128,32,128]{0,2,1:T(8,128)S(1)} %get-tuple-element.24, f32[128,32]{0,1:T(8,128)S(1)} %get-tuple-element.23), kind=kLoop, calls=%fused_computation.52 | loop fusion | flops 2097152 | bytes 6324224 | tf_op jit(solution)/shard_map/convert.6
  19.4 1.0 copy-done.4
  20.4 0.4 copy-done.5
  20.8 2.8 %fusion.38 = f32[32,256,128]{2,1,0:T(8,128)} fusion(bf16[128,32,128]{0,2,1:T(8,128)(2,1)S(1)} %get-tuple-element.29, bf16[128,32,128]{0,2,1:T(8,128)(2,1)S(1)} %get-tuple-element.30, pred[128]{0:T(512)(128)(4,1)S(1)} %add_compare_fusion, bf16[128,32,128]{2,1,0:T(8,128)(2,1)S(1)} %bitcast.143), kind=kOutput, calls=%fused_computation.58 | convolution fusion | flops 273678336 | bytes 7340160 | tf_op jit(solution)/shard_map/shf,she->hfe/dot_general | solution.py:54
  24.3 0.6 fusion.58
  25.4 0.6 bitcast_dynamic-update-slice_fusion.1
  26.1 8.9 %all-reduce.4 = (s32[8]{0:T(128)S(1)}, s32[4]{0:T(128)S(1)}) all-reduce(s32[8]{0:T(128)S(1)} %get-tuple-element.8, s32[4]{0:T(128)S(1)} %bitcast_dynamic-update-slice_fusion.1), channel_id=1, replica_groups=mesh['group'=8,'dp'=4] {'dp'}, use_global_device_ids=true, to_apply=%add | all-reduce | flops 12 | bytes 96
  35.0 2.2 %copy.94 = bf16[32,8,32,128]{3,2,1,0:T(8,128)(2,1)S(1)} copy(bf16[32,8,32,128]{3,1,2,0:T(8,128)(2,1)} %bitcast.137) | data formatting | bytes 4194304
  37.2 3.4 %copy.93 = bf16[32,8,32,128]{3,2,1,0:T(8,128)(2,1)} copy(bf16[32,8,32,128]{3,1,2,0:T(8,128)(2,1)} %bitcast.138) | data formatting | bytes 4194304
  40.6 1.8 copy.95
  43.3 0.6 bitcast_dynamic-update-slice_fusion
  44.5 2.4 %convert_reduce_fusion = f32[32,256]{1,0:T(8,128)S(1)} fusion(bf16[128,32,128]{0,2,1:T(8,128)(2,1)} %copy-done.4, bf16[128,32,128]{0,2,1:T(8,128)(2,1)} %copy-done.5, pred[128]{0:T(512)(128)(4,1)S(1)} %add_compare_fusion), kind=kLoop, calls=%fused_computation.30 | loop fusion | flops 7331840 | bytes 2130048 | tf_op jit(solution)/shard_map/reduce_sum | solution.py:57
  46.9 16.8 %all-reduce.5 = (bf16[32,256]{1,0:T(8,128)(2,1)S(1)}, f32[4]{0:T(128)S(1)}) all-reduce(f32[32,256]{1,0:T(8,128)S(1)} %convert_reduce_fusion, f32[4]{0:T(128)S(1)} %bitcast_dynamic-update-slice_fusion), channel_id=3, replica_groups=mesh['group'=8,'dp'=4] {'dp'}, use_global_device_ids=true, to_apply=%region_15.16.clone | all-reduce | flops 8196 | bytes 49184
  63.7 8.6 %all_gather.17 = bf16[32,256]{1,0:T(8,128)(2,1)S(1)} all-gather(bf16[8,256]{1,0:T(8,128)(2,1)S(1)} %dynamic-slice_convert_fusion), channel_id=1, replica_groups=mesh['group'=8,'dp'=4] {'dp'}, dimensions={0}, use_global_device_ids=true | all-gather | bytes 20480 | tf_op jit(solution)/shard_map/all_gather | solution.py:66
  72.5 3.2 %fusion.31 = f32[32,128,256]{2,1,0:T(8,128)S(1)} fusion(bf16[32,128,128]{2,1,0:T(8,128)(2,1)} %param.20, bf16[256,32,128]{2,1,0:T(8,128)(2,1)} %bitcast.134), kind=kOutput, calls=%fused_computation.50 | convolution fusion | flops 268435456 | bytes 7340032 | tf_op jit(solution)/shard_map/thd,hdf->thf/dot_general | solution.py:10
  75.7 4.0 %fusion.61 = (f32[256,32]{0,1:T(8,128)S(1)}, f32[256,32,128]{0,2,1:T(8,128)S(1)}) fusion(f32[32,128,256]{2,1,0:T(8,128)S(1)} %fusion.31), kind=kOutput, calls=%fused_computation.100 | output fusion | flops 4194431 | bytes 8421376 | tf_op jit(solution)/shard_map/sub | solution.py:12
  79.7 3.9 %fusion.62 = (f32[256,32]{0,1:T(8,128)S(1)}, f32[256,32,128]{0,2,1:T(8,128)S(1)}) fusion(f32[32,128,256]{2,1,0:T(8,128)S(1)} %fusion.31), kind=kOutput, calls=%fused_computation.101 | output fusion | flops 2097279 | bytes 8421376 | tf_op jit(solution)/shard_map/sub | solution.py:12
  83.7 1.2 divide_convert_fusion.2
  84.9 0.7 fusion.37
  85.6 1.4 fusion.29
  87.0 2.0 %copy-done.2 = f32[32,128,256]{2,1,0:T(8,128)} copy-done((f32[32,128,256]{2,1,0:T(8,128)}, f32[32,128,256]{2,1,0:T(8,128)S(1)}, u32[]{:S(2)}) %copy-start.2) | copy-done | bytes 4194328
  88.9 3.0 %fusion.59 = (f32[256,32]{0,1:T(8,128)S(1)}, f32[256,32,128]{0,2,1:T(8,128)}) fusion(f32[32,128,256]{2,1,0:T(8,128)S(1)} %fusion.29), kind=kOutput, calls=%fused_computation.98 | output fusion | flops 4194431 | bytes 8421376 | tf_op jit(solution)/shard_map/sub | solution.py:12
  92.0 2.1 %convert_element_type.44 = bf16[8,256,128]{2,1,0:T(8,128)(2,1)} convert(f32[8,256,128]{2,1,0:T(8,128)} %reduce-scatter.2.cloned.1.call-done) | non-fusion elementwise | flops 262144 | bytes 1572864 | tf_op jit(solution)/shard_map/convert_element_type | solution.py:65
  94.1 4.4 %fusion.60 = (f32[256,32]{0,1:T(8,128)S(1)}, f32[256,32,128]{0,2,1:T(8,128)S(1)}) fusion(f32[32,128,256]{2,1,0:T(8,128)} %copy-done.2), kind=kOutput, calls=%fused_computation.99 | output fusion | flops 2097279 | bytes 8421376 | tf_op jit(solution)/shard_map/sub | solution.py:12
  98.5 0.2 copy-done.3
  98.8 3.2 %divide_convert_fusion = (bf16[256,32,128]{0,2,1:T(8,128)(2,1)}, bf16[256,32,128]{0,2,1:T(8,128)(2,1)}) fusion(f32[256,32,128]{0,2,1:T(8,128)S(1)} %copy-done.3, f32[256,32]{0,1:T(8,128)S(1)} %get-tuple-element.11, f32[256,32,128]{0,2,1:T(8,128)S(1)} %get-tuple-element.14, f32[256,32]{0,1:T(8,128)S(1)} %get-tuple-element.13), kind=kLoop, calls=%fused_computation.32 | loop fusion | flops 4194304 | bytes 12648448 | tf_op jit(solution)/shard_map/convert.2
  102.0 5.3 %select_reduce_fusion = (f32[32,256]{1,0:T(8,128)S(1)}, bf16[32,256,256]{1,2,0:T(8,128)(2,1)}) fusion(pred[256,256]{0,1:T(8,128)(4,1)S(1)} %iota_compare_fusion, bf16[256,32,128]{0,2,1:T(8,128)(2,1)} %get-tuple-element.25, bf16[256,32,128]{0,2,1:T(8,128)(2,1)} %get-tuple-element.26, bf16[256,32,128]{0,2,1:T(8,128)(2,1)S(1)} %copy-done.9, ...), kind=kOutput, calls=%fused_computation.6 | convolution fusion | flops 1096802304 | bytes 12681216 | tf_op jit(solution)/shard_map/thf,shf->hts/dot_general | solution.py:70
  107.3 5.8 %fusion.6 = f32[32,256,128]{1,2,0:T(8,128)} fusion(bf16[32,256,256]{1,2,0:T(8,128)(2,1)} %get-tuple-element.20, pred[256,256]{0,1:T(8,128)(4,1)S(1)} %iota_compare_fusion, bf16[256,32,128]{2,1,0:T(8,128)(2,1)S(1)} %bitcast.140), kind=kOutput, calls=%fused_computation.10 | convolution fusion | flops 538968064 | bytes 10551296 | tf_op jit(solution)/shard_map/hts,she->the/dot_general | solution.py:73
  113.1 16.5 %all-gather.2.cloned.1.call-done = bf16[32,256,128]{2,1,0:T(8,128)(2,1)} async-done(((bf16[8,256,128]{2,1,0:T(8,128)(2,1)}), bf16[32,256,128]{2,1,0:T(8,128)(2,1)}) %all-gather.2.cloned.1.call-update) | async-done | bytes 2097168 | tf_op jit(solution)/shard_map/all_gather | solution.py:65
  129.6 5.1 %fusion.13 = bf16[256,32,128]{0,2,1:T(8,128)(2,1)S(1)} fusion(f32[32,256,128]{1,2,0:T(8,128)} %fusion.6, f32[256,32]{0,1:T(8,128)S(1)} %add_bitcast_fusion, pred[256]{0:T(512)(128)(4,1)S(1)} %iota_compare_fusion.1, bf16[32,256,128]{2,1,0:T(8,128)(2,1)} %all-gather.2.cloned.1.call-done, bf16[256,32,128]{0,2,1:T(8,128)(2,1)} %copy-done.8, ...), kind=kOutput, calls=%fused_computation.19 | convolution fusion | flops 551550976 | bytes 12615936 | tf_op jit(solution)/shard_map/thf,hfe->the/dot_general | solution.py:17
  134.7 3.3 %reshape.185 = bf16[4,64,4096]{1,0,2:T(4,128)(2,1)} reshape(bf16[256,32,128]{0,2,1:T(8,128)(2,1)S(1)} %fusion.13) | data formatting | bytes 4194304 | tf_op jit(solution)/shard_map/reshape | solution.py:81
  138.0 6.6 %copy.74 = bf16[4,64,4096]{2,0,1:T(4,128)(2,1)S(1)} copy(bf16[4,64,4096]{1,0,2:T(4,128)(2,1)} %reshape.185) | data formatting | bytes 4194304 | tf_op jit(solution)/shard_map/reshape | solution.py:81
  144.6 1.2 convolution_convert_fusion
  145.8 2.5 %copy.75 = bf16[4,64,4096]{2,1,0:T(8,128)(2,1)} copy(bf16[4,64,4096]{2,0,1:T(4,128)(2,1)S(1)} %convolution_convert_fusion) | data formatting | bytes 4194304 | tf_op jit(solution)/shard_map/convert_element_type | solution.py:98
  148.3 3.6 %all-to-all-start = ((bf16[4,64,4096]{2,1,0:T(8,128)(2,1)}), bf16[4,64,4096]{2,1,0:T(8,128)(2,1)S(1)}, u32[]{:S(2)}, u32[]{:S(2)}) async-start(bf16[4,64,4096]{2,1,0:T(8,128)(2,1)} %copy.75), calls=%async_computation.1 | async-start | bytes 4194304 | tf_op jit(solution)/shard_map/all_to_all | solution.py:99
  152.0 0.6 reduce_sum.117
  153.2 0.6 multiply_reduce_fusion
  153.8 16.8 %psum.7 = f32[]{:T(128)} all-reduce(f32[]{:T(128)} %multiply_reduce_fusion), channel_id=1, replica_groups=mesh['group'=8,'dp'=4] {'group'}, use_global_device_ids=true, to_apply=%region_20.21 | all-reduce | flops 1 | bytes 8 | tf_op jit(solution)/shard_map/psum | solution.py:106
  171.3 0.2 select_reduce_fusion.1
  171.8 0.6 select_n.62
  172.4 4.5 %all-to-all-done = bf16[4,64,4096]{2,1,0:T(8,128)(2,1)S(1)} async-done(((bf16[4,64,4096]{2,1,0:T(8,128)(2,1)}), bf16[4,64,4096]{2,1,0:T(8,128)(2,1)S(1)}, u32[]{:S(2)}, u32[]{:S(2)}) %all-to-all-start) | async-done | bytes 2097184 | tf_op jit(solution)/shard_map/all_to_all | solution.py:99
  176.9 1.9 %convolution_convert_fusion.1 = bf16[2,64,4096]{2,0,1:T(2,128)(2,1)S(1)} fusion(bf16[4,64,4096]{2,1,0:T(8,128)(2,1)S(1)} %all-to-all-done, s32[2]{0:T(128)S(1)} %get-tuple-element.7), kind=kOutput, calls=%fused_computation.9 | convolution fusion | flops 4718600 | bytes 3145736 | tf_op jit(solution)/shard_map/jd,dbe->jbe/dot_general | solution.py:100
  178.8 1.6 copy.77
  (47 shorter events, 0.9 us)
Async XLA Ops:
  7.2 1.6 copy-start
  7.2 84.8 %reduce-scatter.2.cloned.1.call-start = ((), (), s32[]{:S(2)}) async-start(), calls=%async_computation.2 | async-start | bytes 5242880 | tf_op jit(solution)/shard_map/reduce_scatter | solution.py:61
  17.1 3.6 %copy-start.12 = (bf16[16,8,32,128]{3,2,1,0:T(8,128)(2,1)S(1)}, bf16[16,8,32,128]{3,2,1,0:T(8,128)(2,1)}, u32[]{:S(2)}) copy-start(bf16[16,8,32,128]{3,2,1,0:T(8,128)(2,1)} %copy.92) | copy-start | bytes 3145732
  19.4 1.0 copy-start.4
  19.4 1.3 copy-start.5
  20.8 3.5 %copy-start.13 = (u32[32]{0:T(128)S(1)}, u32[32]{0:T(128)}, u32[]{:S(2)}) copy-start(u32[32]{0:T(128)} %constant.66) | copy-start | bytes 388
  20.8 5.2 %copy-start.14 = (s32[1,2]{1,0:T(1,128)S(1)}, s32[1,2]{1,0:T(1,128)}, u32[]{:S(2)}) copy-start(s32[1,2]{1,0:T(1,128)} %param.18) | copy-start | bytes 28
  23.5 106.1 %all-gather.2.cloned.1.call-start = ((), (), s32[]{:S(2)}) async-start(), calls=%async_computation.3 | async-start | bytes 2621440 | tf_op jit(solution)/shard_map/all_gather | solution.py:65
  35.0 5.7 %copy-start.6 = (bf16[1,256,4096]{2,1,0:T(8,128)(2,1)S(1)}, bf16[1,256,4096]{2,1,0:T(8,128)(2,1)}, u32[]{:S(2)}) copy-start(bf16[1,256,4096]{2,1,0:T(8,128)(2,1)} %param.13) | copy-start | bytes 6291460
  84.9 2.0 %copy-start.8 = (bf16[256,32,128]{0,2,1:T(8,128)(2,1)}, bf16[256,32,128]{0,2,1:T(8,128)(2,1)S(1)}, u32[]{:S(2)}) copy-start(bf16[256,32,128]{0,2,1:T(8,128)(2,1)S(1)} %get-tuple-element.27) | copy-start | bytes 6291460
  84.9 2.0 %copy-start.10 = (bf16[256,32,128]{0,2,1:T(8,128)(2,1)}, bf16[256,32,128]{0,2,1:T(8,128)(2,1)S(1)}, u32[]{:S(2)}) copy-start(bf16[256,32,128]{0,2,1:T(8,128)(2,1)S(1)} %get-tuple-element.28) | copy-start | bytes 6291460
  86.9 2.0 %copy-start.2 = (f32[32,128,256]{2,1,0:T(8,128)}, f32[32,128,256]{2,1,0:T(8,128)S(1)}, u32[]{:S(2)}) copy-start(f32[32,128,256]{2,1,0:T(8,128)S(1)} %fusion.29) | copy-start | bytes 12582916
  94.1 4.6 %copy-start.3 = (f32[256,32,128]{0,2,1:T(8,128)S(1)}, f32[256,32,128]{0,2,1:T(8,128)}, u32[]{:S(2)}) copy-start(f32[256,32,128]{0,2,1:T(8,128)} %get-tuple-element.12) | copy-start | bytes 12582916
  98.8 3.2 %copy-start.9 = (bf16[256,32,128]{0,2,1:T(8,128)(2,1)S(1)}, bf16[256,32,128]{0,2,1:T(8,128)(2,1)}, u32[]{:S(2)}) copy-start(bf16[256,32,128]{0,2,1:T(8,128)(2,1)} %copy-done.8) | copy-start | bytes 6291460
  98.8 3.2 %copy-start.11 = (bf16[256,32,128]{0,2,1:T(8,128)(2,1)S(1)}, bf16[256,32,128]{0,2,1:T(8,128)(2,1)}, u32[]{:S(2)}) copy-start(bf16[256,32,128]{0,2,1:T(8,128)(2,1)} %copy-done.10) | copy-start | bytes 6291460
  102.0 5.3 %copy-start.7 = (bf16[32,8,32,128]{3,2,1,0:T(8,128)(2,1)S(1)}, bf16[32,8,32,128]{3,2,1,0:T(8,128)(2,1)}, u32[]{:S(2)}) copy-start(bf16[32,8,32,128]{3,2,1,0:T(8,128)(2,1)} %copy.95) | copy-start | bytes 6291460
  148.3 28.6 %all-to-all-start = ((bf16[4,64,4096]{2,1,0:T(8,128)(2,1)}), bf16[4,64,4096]{2,1,0:T(8,128)(2,1)S(1)}, u32[]{:S(2)}, u32[]{:S(2)}) async-start(bf16[4,64,4096]{2,1,0:T(8,128)(2,1)} %copy.75), calls=%async_computation.1 | async-start | bytes 4194304 | tf_op jit(solution)/shard_map/all_to_all | solution.py:99
  152.0 28.4 %copy-start.1 = (bf16[32,128,128]{2,1,0:T(8,128)(2,1)S(1)}, bf16[32,128,128]{2,1,0:T(8,128)(2,1)}, u32[]{:S(2)}) copy-start(bf16[32,128,128]{2,1,0:T(8,128)(2,1)} %param.21) | copy-start | bytes 3145732
Sparse Core Ops, SparseCore 0:
  23.7 56.5 reduce-scatter.1
  94.2 35.3 all-gather.1
where the time goes:
time: 188 us; the launch traced here: 187 us
  blocking collectives  51.1 us (27%)
  local copies, waits for them, and re-layouts  31.5 us (17%)
  matrix products  30.7 us (16%)
  other arithmetic  30.3 us (16%)
  waiting for transfers between devices  21.1 us (11%)
  between operations  18.8 us (10%)
  starting transfers between devices  3.69 us (2%)
    unnamed x2, blocking collectives  25.6 us
    psum x1, blocking collectives, body(): spread = lax.psum(jnp.sum(centred * centred), 'group')  16.8 us
    unnamed x41, local copies, waits for them, and re-layouts  16.8 us
    all_gather x1, waiting for transfers between devices, body(): lax.all_gather(kv_share.astype(jnp.bfloat16), 'dp', axis=0, tiled=True)  16.5 us
    sub x3, other arithmetic, features(): jax.nn.softmax(logits, axis=-1)  10.2 us
    reshape x2, local copies, waits for them, and re-layouts, body(): combined.astype(jnp.bfloat16).reshape(-1, BLK, head_count * head_width)  9.89 us
    all_gather x1, blocking collectives, body(): lax.all_gather(total_share.astype(jnp.bfloat16), 'dp', axis=0, tiled=True)  8.64 us
    sub x2, other arithmetic, features(): jax.nn.softmax(-logits, axis=-1)  7.03 us
  transfers between devices with their start and end apart: 3, of which 2 were waited for; matrix products, arithmetic and copies ran while one was open for 27% of the time, Pallas kernels for 0%

commit v1 on v0

--- a/solution.py
+++ b/solution.py
@@ -62,7 +62,12 @@
         lax.psum_scatter(part_total, "dp", scatter_dimension=0, tiled=True),
     )
     kv_state, key_total = (
-        lax.all_gather(kv_share.astype(jnp.bfloat16), "dp", axis=0, tiled=True),
+        jnp.concatenate(
+            lax.all_to_all(
+                jnp.stack([kv_share.astype(jnp.bfloat16)] * lax.axis_size("dp")), "dp", 0, 0
+            ),
+            axis=0,
+        ),
         lax.all_gather(total_share.astype(jnp.bfloat16), "dp", axis=0, tiled=True),
     )
     prompt_num, prompt_den = state_terms(query_feat, kv_state, key_total)

time: 188 us -> 181 us (0.963)
  waiting for transfers between devices: 21.1 us -> 9.08 us
  starting transfers between devices: 3.69 us -> 7.47 us
  matrix products: 30.7 us -> 32.6 us
  blocking collectives: 51.1 us -> 49.2 us
    all_gather x1 -> x0, waiting for transfers between devices: 16.5 us -> none  [body(): lax.all_gather(kv_share.astype(jnp.bfloat16), 'dp', axis=0, tiled=True)]
    all_to_all x0 -> x1, waiting for transfers between devices: none -> 4.64 us  [body(): lax.all_to_all(jnp.stack([kv_share.astype(jnp.bfloat16)] * lax.axis_size(...]
    all_to_all x0 -> x1, starting transfers between devices: none -> 3.83 us  [body(): lax.all_to_all(jnp.stack([kv_share.astype(jnp.bfloat16)] * lax.axis_size(...]
    dot_general x1, matrix products: 5.31 us -> 7.41 us  [body(): jnp.einsum('thf,shf->hts', query_feat, key_feat, preferred_element_type=j...]
    psum x1, blocking collectives: 16.8 us -> 14.8 us  [body(): spread = lax.psum(jnp.sum(centred * centred), 'group')]
    unnamed x41 -> x35, local copies, waits for them, and re-layouts: 16.8 us -> 16.3 us
  transfers between devices with their start and end apart: 3 -> 3, of which waited for: 2 -> 2; matrix products, arithmetic and copies ran while one was open for 27% -> 30% of each run, Pallas kernels for 0% -> 0%
where the time goes in v1:
time: 181 us; the launch traced here: 180 us
  blocking collectives  49.2 us (27%)
  local copies, waits for them, and re-layouts  32.6 us (18%)
  matrix products  32.6 us (18%)
  other arithmetic  29.9 us (17%)
  between operations  19 us (10%)
  waiting for transfers between devices  9.08 us (5%)
  starting transfers between devices  7.47 us (4%)
    unnamed x2, blocking collectives  25.6 us
    unnamed x35, local copies, waits for them, and re-layouts  16.3 us
    psum x1, blocking collectives, body(): spread = lax.psum(jnp.sum(centred * centred), 'group')  14.8 us
    sub x3, other arithmetic, features(): jax.nn.softmax(logits, axis=-1)  9.75 us
    reshape x2, local copies, waits for them, and re-layouts, body(): combined.astype(jnp.bfloat16).reshape(-1, BLK, head_count * head_width)  9.66 us
    all_gather x1, blocking collectives, body(): lax.all_gather(total_share.astype(jnp.bfloat16), 'dp', axis=0, tiled=True)  8.76 us
    sub x2, other arithmetic, features(): jax.nn.softmax(-logits, axis=-1)  7.99 us
    dot_general x1, matrix products, body(): jnp.einsum('thf,shf->hts', query_feat, key_feat, preferred_element_type=j...  7.41 us
  transfers between devices with their start and end apart: 3, of which 2 were waited for; matrix products, arithmetic and copies ran while one was open for 30% of the time, Pallas kernels for 0%

profile of v1, /device:TPU:0, one launch (start us, length us, event | category | flops | bytes accessed | tf_op | source)
XLA Modules:
  0.0 179.8 jit_solution(11901757053926692517)
XLA Ops:
  7.2 1.5 copy.94
  8.8 2.4 %fusion.63 = (f32[128,32]{0,1:T(8,128)S(1)}, f32[128,32,128]{0,2,1:T(8,128)}) fusion(bf16[32,128,128]{2,1,0:T(8,128)(2,1)S(1)} %copy-done, bf16[128,32,128]{2,1,0:T(8,128)(2,1)S(1)} %bitcast.136), kind=kOutput, calls=%fused_computation.102 | convolution fusion | flops 135790720 | bytes 4210688 | tf_op jit(solution)/shard_map/sub | solution.py:12
  11.2 0.9 fusion.40
  12.1 1.9 %fusion.66 = (f32[128,32]{0,1:T(8,128)S(1)}, f32[128,32,128]{0,2,1:T(8,128)S(1)}) fusion(f32[32,128,128]{2,1,0:T(8,128)S(1)} %fusion.40), kind=kOutput, calls=%fused_computation.103 | output fusion | flops 1048703 | bytes 4210688 | tf_op jit(solution)/shard_map/sub | solution.py:12
  14.6 2.5 %copy.95 = bf16[16,8,32,128]{3,2,1,0:T(8,128)(2,1)} copy(bf16[16,8,32,128]{3,1,2,0:T(8,128)(2,1)} %bitcast.144) | data formatting | bytes 2097152
  17.1 2.3 %divide_convert_fusion.4 = (bf16[128,32,128]{0,2,1:T(8,128)(2,1)S(1)}, bf16[128,32,128]{0,2,1:T(8,128)(2,1)S(1)}) fusion(f32[128,32,128]{0,2,1:T(8,128)} %get-tuple-element.22, f32[128,32]{0,1:T(8,128)S(1)} %get-tuple-element.21, f32[128,32,128]{0,2,1:T(8,128)S(1)} %get-tuple-element.24, f32[128,32]{0,1:T(8,128)S(1)} %get-tuple-element.23), kind=kLoop, calls=%fused_computation.52 | loop fusion | flops 2097152 | bytes 6324224 | tf_op jit(solution)/shard_map/convert.6
  19.4 1.0 copy-done.2
  20.4 0.4 copy-done.3
  20.8 2.7 %fusion.38 = f32[32,256,128]{2,1,0:T(8,128)} fusion(bf16[128,32,128]{0,2,1:T(8,128)(2,1)S(1)} %get-tuple-element.29, bf16[128,32,128]{0,2,1:T(8,128)(2,1)S(1)} %get-tuple-element.30, pred[128]{0:T(512)(128)(4,1)S(1)} %add_compare_fusion, bf16[128,32,128]{2,1,0:T(8,128)(2,1)S(1)} %bitcast.145), kind=kOutput, calls=%fused_computation.58 | convolution fusion | flops 273678336 | bytes 7340160 | tf_op jit(solution)/shard_map/shf,she->hfe/dot_general | solution.py:54
  24.1 0.7 fusion.58
  25.5 0.7 bitcast_dynamic-update-slice_fusion.1
  26.4 8.9 %all-reduce.4 = (s32[8]{0:T(128)S(1)}, s32[4]{0:T(128)S(1)}) all-reduce(s32[8]{0:T(128)S(1)} %get-tuple-element.8, s32[4]{0:T(128)S(1)} %bitcast_dynamic-update-slice_fusion.1), channel_id=1, replica_groups=mesh['group'=8,'dp'=4] {'dp'}, use_global_device_ids=true, to_apply=%add | all-reduce | flops 12 | bytes 96
  35.2 2.2 %copy.97 = bf16[32,8,32,128]{3,2,1,0:T(8,128)(2,1)S(1)} copy(bf16[32,8,32,128]{3,1,2,0:T(8,128)(2,1)} %bitcast.138) | data formatting | bytes 4194304
  37.4 3.4 %copy.96 = bf16[32,8,32,128]{3,2,1,0:T(8,128)(2,1)} copy(bf16[32,8,32,128]{3,1,2,0:T(8,128)(2,1)} %bitcast.139) | data formatting | bytes 4194304
  40.9 1.9 %copy.98 = bf16[32,8,32,128]{3,2,1,0:T(8,128)(2,1)} copy(bf16[32,8,32,128]{3,1,2,0:T(8,128)(2,1)S(1)} %bitcast.140) | data formatting | bytes 4194304
  43.6 0.7 bitcast_dynamic-update-slice_fusion
  45.0 2.2 %convert_reduce_fusion = f32[32,256]{1,0:T(8,128)S(1)} fusion(bf16[128,32,128]{0,2,1:T(8,128)(2,1)} %copy-done.2, bf16[128,32,128]{0,2,1:T(8,128)(2,1)} %copy-done.3, pred[128]{0:T(512)(128)(4,1)S(1)} %add_compare_fusion), kind=kLoop, calls=%fused_computation.30 | loop fusion | flops 7331840 | bytes 2130048 | tf_op jit(solution)/shard_map/reduce_sum | solution.py:57
  47.2 16.8 %all-reduce.5 = (bf16[32,256]{1,0:T(8,128)(2,1)S(1)}, f32[4]{0:T(128)S(1)}) all-reduce(f32[32,256]{1,0:T(8,128)S(1)} %convert_reduce_fusion, f32[4]{0:T(128)S(1)} %bitcast_dynamic-update-slice_fusion), channel_id=3, replica_groups=mesh['group'=8,'dp'=4] {'dp'}, use_global_device_ids=true, to_apply=%region_15.16.clone | all-reduce | flops 8196 | bytes 49184
  64.0 8.8 %all_gather.13 = bf16[32,256]{1,0:T(8,128)(2,1)S(1)} all-gather(bf16[8,256]{1,0:T(8,128)(2,1)S(1)} %dynamic-slice_convert_fusion), channel_id=1, replica_groups=mesh['group'=8,'dp'=4] {'dp'}, dimensions={0}, use_global_device_ids=true | all-gather | bytes 20480 | tf_op jit(solution)/shard_map/all_gather | solution.py:71
  72.9 3.3 %fusion.31 = f32[32,128,256]{2,1,0:T(8,128)S(1)} fusion(bf16[32,128,128]{2,1,0:T(8,128)(2,1)} %param.20, bf16[256,32,128]{2,1,0:T(8,128)(2,1)} %bitcast.135), kind=kOutput, calls=%fused_computation.50 | convolution fusion | flops 268435456 | bytes 7340032 | tf_op jit(solution)/shard_map/thd,hdf->thf/dot_general | solution.py:10
  76.1 4.0 %fusion.61 = (f32[256,32]{0,1:T(8,128)S(1)}, f32[256,32,128]{0,2,1:T(8,128)S(1)}) fusion(f32[32,128,256]{2,1,0:T(8,128)S(1)} %fusion.31), kind=kOutput, calls=%fused_computation.100 | output fusion | flops 4194431 | bytes 8421376 | tf_op jit(solution)/shard_map/sub | solution.py:12
  80.1 3.9 %fusion.62 = (f32[256,32]{0,1:T(8,128)S(1)}, f32[256,32,128]{0,2,1:T(8,128)S(1)}) fusion(f32[32,128,256]{2,1,0:T(8,128)S(1)} %fusion.31), kind=kOutput, calls=%fused_computation.101 | output fusion | flops 2097279 | bytes 8421376 | tf_op jit(solution)/shard_map/sub | solution.py:12
  84.1 1.2 divide_convert_fusion.2
  85.3 0.7 fusion.37
  86.0 1.4 fusion.29
  87.4 4.0 %fusion.59 = (f32[256,32]{0,1:T(8,128)S(1)}, f32[256,32,128]{0,2,1:T(8,128)S(1)}) fusion(f32[32,128,256]{2,1,0:T(8,128)S(1)} %fusion.29), kind=kOutput, calls=%fused_computation.98 | output fusion | flops 4194431 | bytes 8421376 | tf_op jit(solution)/shard_map/sub | solution.py:12
  91.4 3.9 %fusion.60 = (f32[256,32]{0,1:T(8,128)S(1)}, f32[256,32,128]{0,2,1:T(8,128)S(1)}) fusion(f32[32,128,256]{2,1,0:T(8,128)S(1)} %fusion.29), kind=kOutput, calls=%fused_computation.99 | output fusion | flops 2097279 | bytes 8421376 | tf_op jit(solution)/shard_map/sub | solution.py:12
  95.3 3.2 %divide_convert_fusion = (bf16[256,32,128]{0,2,1:T(8,128)(2,1)}, bf16[256,32,128]{0,2,1:T(8,128)(2,1)}) fusion(f32[256,32,128]{0,2,1:T(8,128)S(1)} %get-tuple-element.12, f32[256,32]{0,1:T(8,128)S(1)} %get-tuple-element.11, f32[256,32,128]{0,2,1:T(8,128)S(1)} %get-tuple-element.14, f32[256,32]{0,1:T(8,128)S(1)} %get-tuple-element.13), kind=kLoop, calls=%fused_computation.32 | loop fusion | flops 4194304 | bytes 12648448 | tf_op jit(solution)/shard_map/convert.2
  98.5 1.3 convert_element_type.44
  100.1 1.6 stack.2
  101.6 3.8 %all-to-all-start = ((bf16[4,8,256,128]{2,3,1,0:T(8,128)(2,1)}), bf16[4,8,256,128]{2,3,1,0:T(8,128)(2,1)S(1)}, u32[]{:S(2)}, u32[]{:S(2)}) async-start(bf16[4,8,256,128]{2,3,1,0:T(8,128)(2,1)} %stack.2), calls=%async_computation.1 | async-start | bytes 4194304 | tf_op jit(solution)/shard_map/all_to_all | solution.py:66
  105.5 7.4 %select_reduce_fusion = (f32[32,256]{1,0:T(8,128)S(1)}, bf16[32,256,256]{1,2,0:T(8,128)(2,1)}) fusion(pred[256,256]{0,1:T(8,128)(4,1)S(1)} %iota_compare_fusion, bf16[256,32,128]{0,2,1:T(8,128)(2,1)} %get-tuple-element.25, bf16[256,32,128]{0,2,1:T(8,128)(2,1)} %get-tuple-element.26, bf16[256,32,128]{0,2,1:T(8,128)(2,1)} %copy-done.7, ...), kind=kOutput, calls=%fused_computation.6 | convolution fusion | flops 1096802304 | bytes 12681216 | tf_op jit(solution)/shard_map/thf,shf->hts/dot_general | solution.py:75
  112.9 5.9 %fusion.6 = f32[32,256,128]{1,2,0:T(8,128)} fusion(bf16[32,256,256]{1,2,0:T(8,128)(2,1)} %get-tuple-element.20, pred[256,256]{0,1:T(8,128)(4,1)S(1)} %iota_compare_fusion, bf16[256,32,128]{2,1,0:T(8,128)(2,1)S(1)} %bitcast.141), kind=kOutput, calls=%fused_computation.10 | convolution fusion | flops 538968064 | bytes 10551296 | tf_op jit(solution)/shard_map/hts,she->the/dot_general | solution.py:78
  118.8 4.6 %all-to-all-done = bf16[4,8,256,128]{2,3,1,0:T(8,128)(2,1)S(1)} async-done(((bf16[4,8,256,128]{2,3,1,0:T(8,128)(2,1)}), bf16[4,8,256,128]{2,3,1,0:T(8,128)(2,1)S(1)}, u32[]{:S(2)}, u32[]{:S(2)}) %all-to-all-start) | async-done | bytes 2097184 | tf_op jit(solution)/shard_map/all_to_all | solution.py:66
  123.5 1.3 copy-done.6
  124.8 4.8 %fusion.13 = bf16[256,32,128]{0,2,1:T(8,128)(2,1)S(1)} fusion(f32[32,256,128]{1,2,0:T(8,128)} %fusion.6, f32[256,32]{0,1:T(8,128)S(1)} %add_bitcast_fusion, pred[256]{0:T(512)(128)(4,1)S(1)} %iota_compare_fusion.1, bf16[32,256,128]{1,2,0:T(8,128)(2,1)} %bitcast.142, bf16[256,32,128]{0,2,1:T(8,128)(2,1)} %copy-done.7, bf16[256,32,128]{0,2,1:T(8,128)(2,1)} %copy-done.8), kind=kOutput, calls=%fused_computation.19 | convolution fusion | flops 551550976 | bytes 12615936 | tf_op jit(solution)/shard_map/thf,hfe->the/dot_general | solution.py:17
  129.6 3.3 %reshape.191 = bf16[4,64,4096]{1,0,2:T(4,128)(2,1)} reshape(bf16[256,32,128]{0,2,1:T(8,128)(2,1)S(1)} %fusion.13) | data formatting | bytes 4194304 | tf_op jit(solution)/shard_map/reshape | solution.py:86
  132.9 6.4 %copy.78 = bf16[4,64,4096]{2,0,1:T(4,128)(2,1)S(1)} copy(bf16[4,64,4096]{1,0,2:T(4,128)(2,1)} %reshape.191) | data formatting | bytes 4194304 | tf_op jit(solution)/shard_map/reshape | solution.py:86
  139.3 1.2 convolution_convert_fusion
  140.5 2.5 %copy.79 = bf16[4,64,4096]{2,1,0:T(8,128)(2,1)} copy(bf16[4,64,4096]{2,0,1:T(4,128)(2,1)S(1)} %convolution_convert_fusion) | data formatting | bytes 4194304 | tf_op jit(solution)/shard_map/convert_element_type | solution.py:103
  143.0 3.6 %all-to-all-start.1 = ((bf16[4,64,4096]{2,1,0:T(8,128)(2,1)}), bf16[4,64,4096]{2,1,0:T(8,128)(2,1)S(1)}, u32[]{:S(2)}, u32[]{:S(2)}) async-start(bf16[4,64,4096]{2,1,0:T(8,128)(2,1)} %copy.79), calls=%async_computation.2 | async-start | bytes 4194304 | tf_op jit(solution)/shard_map/all_to_all | solution.py:104
  146.7 0.6 reduce_sum.117
  147.9 0.6 multiply_reduce_fusion
  148.5 14.8 %psum.7 = f32[]{:T(128)} all-reduce(f32[]{:T(128)} %multiply_reduce_fusion), channel_id=1, replica_groups=mesh['group'=8,'dp'=4] {'group'}, use_global_device_ids=true, to_apply=%region_20.21 | all-reduce | flops 1 | bytes 8 | tf_op jit(solution)/shard_map/psum | solution.py:111
  164.5 0.6 select_n.62
  165.1 4.4 %all-to-all-done.1 = bf16[4,64,4096]{2,1,0:T(8,128)(2,1)S(1)} async-done(((bf16[4,64,4096]{2,1,0:T(8,128)(2,1)}), bf16[4,64,4096]{2,1,0:T(8,128)(2,1)S(1)}, u32[]{:S(2)}, u32[]{:S(2)}) %all-to-all-start.1) | async-done | bytes 2097184 | tf_op jit(solution)/shard_map/all_to_all | solution.py:104
  169.5 1.9 %convolution_convert_fusion.1 = bf16[2,64,4096]{2,0,1:T(2,128)(2,1)S(1)} fusion(bf16[4,64,4096]{2,1,0:T(8,128)(2,1)S(1)} %all-to-all-done.1, s32[2]{0:T(128)S(1)} %get-tuple-element.7), kind=kOutput, calls=%fused_computation.9 | convolution fusion | flops 4718600 | bytes 3145736 | tf_op jit(solution)/shard_map/jd,dbe->jbe/dot_general | solution.py:105
  171.4 1.6 copy.81
  (42 shorter events, 1.2 us)
Async XLA Ops:
  7.2 1.6 copy-start
  7.2 91.3 %reduce-scatter.2.cloned.1.call-start = ((), (), s32[]{:S(2)}) async-start(), calls=%async_computation.3 | async-start | bytes 5242880 | tf_op jit(solution)/shard_map/reduce_scatter | solution.py:61
  17.1 3.6 %copy-start.9 = (bf16[16,8,32,128]{3,2,1,0:T(8,128)(2,1)S(1)}, bf16[16,8,32,128]{3,2,1,0:T(8,128)(2,1)}, u32[]{:S(2)}) copy-start(bf16[16,8,32,128]{3,2,1,0:T(8,128)(2,1)} %copy.95) | copy-start | bytes 3145732
  19.4 1.0 copy-start.2
  19.4 1.3 copy-start.3
  20.7 3.4 %copy-start.10 = (u32[32]{0:T(128)S(1)}, u32[32]{0:T(128)}, u32[]{:S(2)}) copy-start(u32[32]{0:T(128)} %constant.66) | copy-start | bytes 388
  20.7 5.5 %copy-start.11 = (s32[1,2]{1,0:T(1,128)S(1)}, s32[1,2]{1,0:T(1,128)}, u32[]{:S(2)}) copy-start(s32[1,2]{1,0:T(1,128)} %param.18) | copy-start | bytes 28
  35.2 5.7 %copy-start.4 = (bf16[1,256,4096]{2,1,0:T(8,128)(2,1)S(1)}, bf16[1,256,4096]{2,1,0:T(8,128)(2,1)}, u32[]{:S(2)}) copy-start(bf16[1,256,4096]{2,1,0:T(8,128)(2,1)} %param.13) | copy-start | bytes 6291460
  85.3 2.0 %copy-start.7 = (bf16[256,32,128]{0,2,1:T(8,128)(2,1)}, bf16[256,32,128]{0,2,1:T(8,128)(2,1)S(1)}, u32[]{:S(2)}) copy-start(bf16[256,32,128]{0,2,1:T(8,128)(2,1)S(1)} %get-tuple-element.27) | copy-start | bytes 6291460
  85.3 2.0 %copy-start.8 = (bf16[256,32,128]{0,2,1:T(8,128)(2,1)}, bf16[256,32,128]{0,2,1:T(8,128)(2,1)S(1)}, u32[]{:S(2)}) copy-start(bf16[256,32,128]{0,2,1:T(8,128)(2,1)S(1)} %get-tuple-element.28) | copy-start | bytes 6291460
  101.6 21.8 %all-to-all-start = ((bf16[4,8,256,128]{2,3,1,0:T(8,128)(2,1)}), bf16[4,8,256,128]{2,3,1,0:T(8,128)(2,1)S(1)}, u32[]{:S(2)}, u32[]{:S(2)}) async-start(bf16[4,8,256,128]{2,3,1,0:T(8,128)(2,1)} %stack.2), calls=%async_computation.1 | async-start | bytes 4194304 | tf_op jit(solution)/shard_map/all_to_all | solution.py:66
  105.5 7.4 %copy-start.5 = (bf16[32,8,32,128]{3,2,1,0:T(8,128)(2,1)S(1)}, bf16[32,8,32,128]{3,2,1,0:T(8,128)(2,1)}, u32[]{:S(2)}) copy-start(bf16[32,8,32,128]{3,2,1,0:T(8,128)(2,1)} %copy.98) | copy-start | bytes 6291460
  123.5 1.3 copy-start.6
  143.0 26.4 %all-to-all-start.1 = ((bf16[4,64,4096]{2,1,0:T(8,128)(2,1)}), bf16[4,64,4096]{2,1,0:T(8,128)(2,1)S(1)}, u32[]{:S(2)}, u32[]{:S(2)}) async-start(bf16[4,64,4096]{2,1,0:T(8,128)(2,1)} %copy.79), calls=%async_computation.2 | async-start | bytes 4194304 | tf_op jit(solution)/shard_map/all_to_all | solution.py:104
  146.7 26.3 %copy-start.1 = (bf16[32,128,128]{2,1,0:T(8,128)(2,1)S(1)}, bf16[32,128,128]{2,1,0:T(8,128)(2,1)}, u32[]{:S(2)}) copy-start(bf16[32,128,128]{2,1,0:T(8,128)(2,1)} %param.21) | copy-start | bytes 3145732
Sparse Core Ops, SparseCore 0:
  23.6 56.4 reduce-scatter.1
